TPU v7x, 32 devices: a whole 2x2x4 slice. The times are simulated.
32 devices in a mesh: blk: 4 (over x, core), ulysses: 8 (over z, y).
Axes of the slice: x: 2, y: 2, z: 4, core: 2. Of those that a mesh axis runs over, the one named last changes fastest.
Arguments:
- query_rows: bfloat16 [32, 4096, 128], P(None, ('blk', 'ulysses')), may hold values from -160 to 160
- out_grad: bfloat16 [32, 4096, 128], P(None, ('blk', 'ulysses')), may hold values from -6 to 6
- key_rows: bfloat16 [32, 512, 128], P(None, 'blk'), may hold values from -6 to 6
- value_rows: bfloat16 [32, 512, 128], P(None, 'blk'), may hold values from -6 to 6
- routes: int32 [4, 4], replicated, may hold values from 0 to 7
Outputs:
- query_grad: bfloat16 [32, 4096, 128], P(None, ('blk', 'ulysses'))
- key_grad: float32 [32, 512, 128], P(None, ('blk', 'ulysses'))
- value_grad: float32 [32, 512, 128], P(None, ('blk', 'ulysses'))
All inputs are finite; a program needn't handle non-finite values.
Results may differ from a plain program's by a relative error of at most 0.0056.
Values may be sent and summed in bfloat16 or wider, within the bound.
No kernel may reach another device: no remote copies, remote signals or barrier semaphores. Data moves between devices by JAX's collectives and lax.ppermute only.
A program may use at most 64 MiB of HBM per device.

v0:
```python
import math
import jax
import jax.numpy as jnp
from jax import lax
from jax.sharding import PartitionSpec as P

KB = 16


def body(query_rows, out_grad, key_rows, value_rows, routes):
    head_count, token_count, head_dim = query_rows.shape
    group_keys = key_rows.shape[1]
    cycle_size = lax.axis_size("blk")
    group_size = lax.axis_size("ulysses")
    sub_count = max(1, group_size // head_count)
    item_count = head_count * sub_count // group_size
    sub_length = token_count // sub_count
    row_count = group_size * sub_length
    block_count = group_keys // KB
    key_stride = token_count * group_size // group_keys
    score_scale = 1.0 / math.sqrt(head_dim)
    my_group = lax.axis_index("blk")
    my_rank = lax.axis_index("ulysses")
    packed_query = query_rows.reshape(head_count * sub_count, sub_length, head_dim)
    packed_grad = out_grad.reshape(head_count * sub_count, sub_length, head_dim)
    local_query, local_grad = (
        lax.all_to_all(packed_query, "ulysses", split_axis=0, concat_axis=1, tiled=True),
        lax.all_to_all(packed_grad, "ulysses", split_axis=0, concat_axis=1, tiled=True),
    )
    first_head = my_rank * item_count // sub_count
    own_keys = lax.dynamic_slice_in_dim(key_rows, first_head, item_count, 0)
    own_values = lax.dynamic_slice_in_dim(value_rows, first_head, item_count, 0)
    requested = lax.dynamic_index_in_dim(routes, my_group, 1, keepdims=False)
    block_ids = jnp.arange(block_count, dtype=jnp.int32)
    block_keys = own_keys.reshape(item_count, block_count, KB, head_dim)
    block_values = own_values.reshape(item_count, block_count, KB, head_dim)
    far_keys, far_values = (
        lax.all_to_all(
            jnp.take(block_keys, requested, axis=1), "blk", split_axis=1, concat_axis=1, tiled=True
        ),
        lax.all_to_all(
            jnp.take(block_values, requested, axis=1),
            "blk",
            split_axis=1,
            concat_axis=1,
            tiled=True,
        ),
    )
    near_keys = jnp.concatenate(
        [own_keys, far_keys.reshape(item_count, cycle_size * KB, head_dim)], axis=1
    )
    near_values = jnp.concatenate(
        [own_values, far_values.reshape(item_count, cycle_size * KB, head_dim)], axis=1
    )
    near_count = near_keys.shape[1]
    item_sub = (my_rank * item_count + jnp.arange(item_count, dtype=jnp.int32)) % sub_count
    far_visible = jnp.repeat(jnp.arange(cycle_size, dtype=jnp.int32) < my_group, KB)
    own_offsets = jnp.arange(group_keys, dtype=jnp.int32) * key_stride
    block_rows = 1024

    def attend(row_block, carried):
        query_out, key_acc, value_acc = carried
        row_start = row_block * block_rows
        queries = lax.dynamic_slice_in_dim(local_query, row_start, block_rows, 1)
        grad_rows = lax.dynamic_slice_in_dim(local_grad, row_start, block_rows, 1)
        row_ids = row_start + jnp.arange(block_rows, dtype=jnp.int32)
        positions = (
            row_ids[None, :] // sub_length * token_count
            + item_sub[:, None] * sub_length
            + row_ids[None, :] % sub_length
        )
        own_visible = own_offsets[None, None, :] <= positions[:, :, None]
        visible = jnp.concatenate(
            [
                own_visible,
                jnp.broadcast_to(far_visible, (item_count, block_rows, far_visible.shape[0])),
            ],
            axis=2,
        )
        scores = (
            jnp.einsum("ird,ikd->irk", queries, near_keys, preferred_element_type=jnp.float32)
            * score_scale
        )
        row_max = jnp.max(jnp.where(visible, scores, -jnp.inf), axis=-1, keepdims=True)
        expsum = jnp.where(visible, jnp.exp(scores - row_max), 0.0)
        weights = expsum / jnp.sum(expsum, axis=-1, keepdims=True)
        weights_half = weights.astype(jnp.bfloat16)
        attended = jnp.einsum(
            "irk,ikd->ird", weights_half, near_values, preferred_element_type=jnp.float32
        )
        delta_rows = jnp.sum(grad_rows.astype(jnp.float32) * attended, axis=-1, keepdims=True)
        dweights = jnp.einsum(
            "ird,ikd->irk", grad_rows, near_values, preferred_element_type=jnp.float32
        )
        dscore = (weights * (dweights - delta_rows)).astype(jnp.bfloat16)
        query_part = (
            jnp.einsum("irk,ikd->ird", dscore, near_keys, preferred_element_type=jnp.float32)
            * score_scale
        ).astype(jnp.bfloat16)
        key_acc = (
            key_acc
            + jnp.einsum("irk,ird->ikd", dscore, queries, preferred_element_type=jnp.float32)
            * score_scale
        )
        value_acc = value_acc + jnp.einsum(
            "irk,ird->ikd", weights_half, grad_rows, preferred_element_type=jnp.float32
        )
        query_out = lax.dynamic_update_slice_in_dim(query_out, query_part, row_start, 1)
        return (query_out, key_acc, value_acc)

    start_state = (
        jnp.zeros((item_count, row_count, head_dim), jnp.bfloat16),
        jnp.zeros((item_count, near_count, head_dim), jnp.float32),
        jnp.zeros((item_count, near_count, head_dim), jnp.float32),
    )
    query_out, key_acc, value_acc = lax.fori_loop(0, row_count // block_rows, attend, start_state)
    own_key_grad = key_acc[:, :group_keys]
    own_value_grad = value_acc[:, :group_keys]
    far_key_grad = key_acc[:, group_keys:].reshape(item_count, cycle_size, KB, head_dim)
    far_value_grad = value_acc[:, group_keys:].reshape(item_count, cycle_size, KB, head_dim)
    back_keys, back_values = (
        lax.all_to_all(far_key_grad, "blk", split_axis=1, concat_axis=1, tiled=True),
        lax.all_to_all(far_value_grad, "blk", split_axis=1, concat_axis=1, tiled=True),
    )
    placer = (requested[:, None] == block_ids[None, :]).astype(jnp.float32)
    added_keys = jnp.einsum(
        "gb,igkd->ibkd", placer, back_keys, precision=lax.Precision.HIGHEST
    ).reshape(item_count, group_keys, head_dim)
    added_values = jnp.einsum(
        "gb,igkd->ibkd", placer, back_values, precision=lax.Precision.HIGHEST
    ).reshape(item_count, group_keys, head_dim)
    key_share = (own_key_grad + added_keys).astype(jnp.bfloat16)
    value_share = (own_value_grad + added_values).astype(jnp.bfloat16)
    query_back, key_back, value_back = (
        lax.all_to_all(query_out, "ulysses", split_axis=1, concat_axis=0, tiled=True),
        lax.all_to_all(key_share, "ulysses", split_axis=1, concat_axis=0, tiled=True),
        lax.all_to_all(value_share, "ulysses", split_axis=1, concat_axis=0, tiled=True),
    )
    query_grad = query_back.reshape(head_count, token_count, head_dim)
    key_grad = jnp.sum(
        key_back.astype(jnp.float32).reshape(head_count, sub_count, -1, head_dim), axis=1
    )
    value_grad = jnp.sum(
        value_back.astype(jnp.float32).reshape(head_count, sub_count, -1, head_dim), axis=1
    )
    return (query_grad, key_grad, value_grad)


def solution(mesh):
    return jax.shard_map(
        body,
        mesh=mesh,
        in_specs=(
            P(None, ("blk", "ulysses"), None),
            P(None, ("blk", "ulysses"), None),
            P(None, "blk", None),
            P(None, "blk", None),
            P(),
        ),
        out_specs=(
            P(None, ("blk", "ulysses"), None),
            P(None, ("blk", "ulysses"), None),
            P(None, ("blk", "ulysses"), None),
        ),
        check_vma=False,
    )
```

profile of v0, /device:TPU:0, one launch (start us, length us, event | category | flops | bytes accessed | tf_op | source)
XLA Modules:
  0.0 155.4 jit_solution(3819428733041253633)
XLA Ops:
  1.5 1.0 constant_dynamic-slice_fusion
  3.8 8.2 %all_to_all.92 = bf16[4,4,16,128]{3,2,0,1:T(8,128)(2,1)S(1)} all-to-all(bf16[4,4,16,128]{3,2,0,1:T(8,128)(2,1)S(1)} %get-tuple-element.29), channel_id=1, replica_groups=mesh['blk'=4,'ulysses'=8] {'blk'}, dimensions={1} | all-to-all | bytes 131072 | tf_op jit(solution)/shard_map/all_to_all | solution.py:38
  11.9 6.5 %all_to_all.93 = bf16[4,4,16,128]{3,2,0,1:T(8,128)(2,1)S(1)} all-to-all(bf16[4,4,16,128]{3,2,0,1:T(8,128)(2,1)S(1)} %get-tuple-element.28), channel_id=1, replica_groups=mesh['blk'=4,'ulysses'=8] {'blk'}, dimensions={1} | all-to-all | bytes 131072 | tf_op jit(solution)/shard_map/all_to_all | solution.py:41
  18.4 31.4 %all_to_all.94 = bf16[32,128,128]{2,1,0:T(8,128)(2,1)S(1)} all-to-all(bf16[32,128,128]{2,1,0:T(8,128)(2,1)} %param.7), channel_id=1, replica_groups=mesh['blk'=4,'ulysses'=8] {'ulysses'}, dimensions={0} | all-to-all | bytes 2097152 | tf_op jit(solution)/shard_map/all_to_all | solution.py:27
  49.8 3.6 %all-to-all-start.3 = ((bf16[32,128,128]{2,1,0:T(8,128)(2,1)}), bf16[32,128,128]{2,1,0:T(8,128)(2,1)S(1)}, u32[]{:S(2)}, u32[]{:S(2)}) async-start(bf16[32,128,128]{2,1,0:T(8,128)(2,1)} %param.8), calls=%async_computation.3 | async-start | bytes 2097152 | tf_op jit(solution)/shard_map/all_to_all | solution.py:28
  53.6 1.0 broadcast_compare_fusion
  55.4 23.6 %all-to-all-done.3 = bf16[32,128,128]{2,1,0:T(8,128)(2,1)S(1)} async-done(((bf16[32,128,128]{2,1,0:T(8,128)(2,1)}), bf16[32,128,128]{2,1,0:T(8,128)(2,1)S(1)}, u32[]{:S(2)}, u32[]{:S(2)}) %all-to-all-start.3) | async-done | bytes 1048608 | tf_op jit(solution)/shard_map/all_to_all | solution.py:28
  79.0 1.0 copy.33
  80.0 4.5 %fusion.40 = (f32[4,1024]{1,0:T(4,128)S(1)}, f32[4,1024,192]{1,2,0:T(8,128)}) fusion(pred[4,1024,128]{1,2,0:T(32,128)(4,1)} %broadcast_compare_fusion, pred[192]{0:T(512)(128)(4,1)S(1)} %pad.5.clone, bf16[4,1024,128]{2,1,0:T(8,128)(2,1)S(1)} %bitcast.73, bf16[4,64,128]{2,1,0:T(8,128)(2,1)S(1)} %bitcast.90, bf16[4,128,128]{2,1,0:T(8,128)(2,1)S(1)} %get-tuple-element.33), kind=kOutput, calls=%fused_computation.69 | convolution fusion | flops 409731264 | bytes 4931776 | tf_op jit(solution)/shard_map/while/body/eval_jaxpr/sub | solution.py:85
  84.6 2.4 %fusion.8 = bf16[4,1024,192]{1,2,0:T(8,128)(2,1)S(1)} fusion(f32[4,1024,192]{1,2,0:T(8,128)} %get-tuple-element.31, f32[4,1024]{1,0:T(4,128)S(1)} %get-tuple-element.30), kind=kLoop, calls=%fused_computation.17 | loop fusion | flops 1572864 | bytes 4734976 | tf_op jit(solution)/shard_map/while/body/eval_jaxpr/convert_element_type | solution.py:87
  88.2 3.3 %all-to-all-start.7 = ((f32[4,4,16,128]{3,2,0,1:T(8,128)}), f32[4,4,16,128]{3,2,0,1:T(8,128)S(1)}, u32[]{:S(2)}, u32[]{:S(2)}) async-start(f32[4,4,16,128]{3,2,0,1:T(8,128)} %copy.42), calls=%async_computation.7 | async-start | bytes 262144 | tf_op jit(solution)/shard_map/all_to_all | solution.py:123
  91.6 2.5 %multiply_reduce_fusion = f32[4,1024]{1,0:T(4,128)S(1)} fusion(bf16[4,1024,128]{2,1,0:T(8,128)(2,1)} %bitcast.75, bf16[4,1024,192]{1,2,0:T(8,128)(2,1)S(1)} %fusion.8, bf16[4,64,128]{2,1,0:T(8,128)(2,1)S(1)} %bitcast.92, bf16[4,128,128]{2,1,0:T(8,128)(2,1)S(1)} %copy-done.6), kind=kOutput, calls=%fused_computation.12 | convolution fusion | flops 203288576 | bytes 2834432 | tf_op jit(solution)/shard_map/while/body/eval_jaxpr/irk,ikd->ird/dot_general | solution.py:88
  94.1 2.5 %fusion.1 = bf16[4,1024,192]{1,2,0:T(8,128)(2,1)S(1)} fusion(bf16[4,1024,128]{2,1,0:T(8,128)(2,1)S(1)} %bitcast.77, f32[4,1024]{1,0:T(4,128)S(1)} %multiply_reduce_fusion, f32[4,1024,192]{1,2,0:T(8,128)} %get-tuple-element.31, f32[4,1024]{1,0:T(4,128)S(1)} %get-tuple-element.30, bf16[4,64,128]{2,1,0:T(8,128)(2,1)S(1)} %bitcast.93, ...), kind=kOutput, calls=%fused_computation.4 | convolution fusion | flops 204865536 | bytes 5996544 | tf_op jit(solution)/shard_map/while/body/eval_jaxpr/ird,ikd->irk/dot_general | solution.py:92
  97.9 3.3 %all-to-all-start.5 = ((f32[4,4,16,128]{3,2,0,1:T(8,128)}), f32[4,4,16,128]{3,2,0,1:T(8,128)S(1)}, u32[]{:S(2)}, u32[]{:S(2)}) async-start(f32[4,4,16,128]{3,2,0,1:T(8,128)} %copy.37), calls=%async_computation.5 | async-start | bytes 262144 | tf_op jit(solution)/shard_map/all_to_all | solution.py:122
  102.5 3.3 %all-to-all-done.5 = f32[4,4,16,128]{3,2,0,1:T(8,128)S(1)} async-done(((f32[4,4,16,128]{3,2,0,1:T(8,128)}), f32[4,4,16,128]{3,2,0,1:T(8,128)S(1)}, u32[]{:S(2)}, u32[]{:S(2)}) %all-to-all-start.5) | async-done | bytes 131104 | tf_op jit(solution)/shard_map/all_to_all | solution.py:122
  105.8 3.4 %all-to-all-start.8 = ((bf16[4,128,128]{2,0,1:T(4,128)(2,1)}), bf16[4,128,128]{2,0,1:T(4,128)(2,1)S(1)}, u32[]{:S(2)}, u32[]{:S(2)}) async-start(bf16[4,128,128]{2,0,1:T(4,128)(2,1)} %copy.45), calls=%async_computation.8 | async-start | bytes 262144 | tf_op jit(solution)/shard_map/all_to_all | solution.py:137
  110.5 6.1 %all-to-all-done.8 = bf16[4,128,128]{2,0,1:T(4,128)(2,1)S(1)} async-done(((bf16[4,128,128]{2,0,1:T(4,128)(2,1)}), bf16[4,128,128]{2,0,1:T(4,128)(2,1)S(1)}, u32[]{:S(2)}, u32[]{:S(2)}) %all-to-all-start.8) | async-done | bytes 131104 | tf_op jit(solution)/shard_map/all_to_all | solution.py:137
  116.6 3.4 %all-to-all-start.6 = ((bf16[4,128,128]{2,0,1:T(4,128)(2,1)}), bf16[4,128,128]{2,0,1:T(4,128)(2,1)S(1)}, u32[]{:S(2)}, u32[]{:S(2)}) async-start(bf16[4,128,128]{2,0,1:T(4,128)(2,1)} %copy.40), calls=%async_computation.6 | async-start | bytes 262144 | tf_op jit(solution)/shard_map/all_to_all | solution.py:136
  120.0 1.0 multiply_convert_fusion
  120.9 1.8 %copy.35 = bf16[4,1024,128]{2,0,1:T(4,128)(2,1)} copy(bf16[4,1024,128]{2,1,0:T(8,128)(2,1)S(1)} %multiply_convert_fusion) | data formatting | bytes 2097152 | tf_op jit(solution)/shard_map/while/body/eval_jaxpr/convert_element_type | solution.py:99
  122.7 4.5 %all-to-all-done.6 = bf16[4,128,128]{2,0,1:T(4,128)(2,1)S(1)} async-done(((bf16[4,128,128]{2,0,1:T(4,128)(2,1)}), bf16[4,128,128]{2,0,1:T(4,128)(2,1)S(1)}, u32[]{:S(2)}, u32[]{:S(2)}) %all-to-all-start.6) | async-done | bytes 131104 | tf_op jit(solution)/shard_map/all_to_all | solution.py:136
  127.2 3.6 %all-to-all-start.4 = ((bf16[4,1024,128]{2,0,1:T(4,128)(2,1)}), bf16[4,1024,128]{2,0,1:T(4,128)(2,1)S(1)}, u32[]{:S(2)}, u32[]{:S(2)}) async-start(bf16[4,1024,128]{2,0,1:T(4,128)(2,1)} %copy.35), calls=%async_computation.4 | async-start | bytes 2097152 | tf_op jit(solution)/shard_map/all_to_all | solution.py:135
  132.3 21.9 %all-to-all-done.4 = bf16[4,1024,128]{2,0,1:T(4,128)(2,1)S(1)} async-done(((bf16[4,1024,128]{2,0,1:T(4,128)(2,1)}), bf16[4,1024,128]{2,0,1:T(4,128)(2,1)S(1)}, u32[]{:S(2)}, u32[]{:S(2)}) %all-to-all-start.4) | async-done | bytes 1048608 | tf_op jit(solution)/shard_map/all_to_all | solution.py:135
  154.2 1.2 copy.36
  (55 shorter events, 9.5 us)
Async XLA Ops:
  0.6 0.7 copy-start
  2.5 52.8 %copy-start.5 = (bf16[4,128,128]{2,1,0:T(8,128)(2,1)}, bf16[4,128,128]{2,1,0:T(8,128)(2,1)S(1)}, u32[]{:S(2)}) copy-start(bf16[4,128,128]{2,1,0:T(8,128)(2,1)S(1)} %get-tuple-element.32) | copy-start | bytes 393220
  2.5 77.5 %copy-start.3 = (bf16[4,128,128]{2,1,0:T(8,128)(2,1)}, bf16[4,128,128]{2,1,0:T(8,128)(2,1)S(1)}, u32[]{:S(2)}) copy-start(bf16[4,128,128]{2,1,0:T(8,128)(2,1)S(1)} %get-tuple-element.33) | copy-start | bytes 393220
  49.8 29.2 %all-to-all-start.3 = ((bf16[32,128,128]{2,1,0:T(8,128)(2,1)}), bf16[32,128,128]{2,1,0:T(8,128)(2,1)S(1)}, u32[]{:S(2)}, u32[]{:S(2)}) async-start(bf16[32,128,128]{2,1,0:T(8,128)(2,1)} %param.8), calls=%async_computation.3 | async-start | bytes 2097152 | tf_op jit(solution)/shard_map/all_to_all | solution.py:28
  54.6 29.9 %copy-start.7 = (bf16[4,4,16,128]{3,2,1,0:T(8,128)(2,1)}, bf16[4,4,16,128]{3,2,1,0:T(8,128)(2,1)S(1)}, u32[]{:S(2)}) copy-start(bf16[4,4,16,128]{3,2,1,0:T(8,128)(2,1)S(1)} %copy.30) | copy-start | bytes 196612
  84.5 2.5 %copy-start.1 = (bf16[8,4,128,128]{3,2,0,1:T(8,128)(2,1)S(1)}, bf16[8,4,128,128]{3,2,0,1:T(8,128)(2,1)}, u32[]{:S(2)}) copy-start(bf16[8,4,128,128]{3,2,0,1:T(8,128)(2,1)} %copy.33) | copy-start | bytes 3145732
  84.5 7.1 %copy-start.6 = (bf16[4,128,128]{2,1,0:T(8,128)(2,1)S(1)}, bf16[4,128,128]{2,1,0:T(8,128)(2,1)}, u32[]{:S(2)}) copy-start(bf16[4,128,128]{2,1,0:T(8,128)(2,1)} %copy-done.5) | copy-start | bytes 393220
  84.5 7.1 %copy-start.9 = (bf16[4,4,16,128]{3,2,1,0:T(8,128)(2,1)S(1)}, bf16[4,4,16,128]{3,2,1,0:T(8,128)(2,1)}, u32[]{:S(2)}) copy-start(bf16[4,4,16,128]{3,2,1,0:T(8,128)(2,1)} %copy.32) | copy-start | bytes 196612
  88.2 9.6 %all-to-all-start.7 = ((f32[4,4,16,128]{3,2,0,1:T(8,128)}), f32[4,4,16,128]{3,2,0,1:T(8,128)S(1)}, u32[]{:S(2)}, u32[]{:S(2)}) async-start(f32[4,4,16,128]{3,2,0,1:T(8,128)} %copy.42), calls=%async_computation.7 | async-start | bytes 262144 | tf_op jit(solution)/shard_map/all_to_all | solution.py:123
  91.6 2.5 %copy-start.2 = (bf16[8,4,128,128]{3,2,0,1:T(8,128)(2,1)S(1)}, bf16[8,4,128,128]{3,2,0,1:T(8,128)(2,1)}, u32[]{:S(2)}) copy-start(bf16[8,4,128,128]{3,2,0,1:T(8,128)(2,1)} %copy.33) | copy-start | bytes 3145732
  97.2 22.8 %copy-start.4 = (bf16[4,128,128]{2,1,0:T(8,128)(2,1)S(1)}, bf16[4,128,128]{2,1,0:T(8,128)(2,1)}, u32[]{:S(2)}) copy-start(bf16[4,128,128]{2,1,0:T(8,128)(2,1)} %copy-done.3) | copy-start | bytes 393220
  97.2 22.8 %copy-start.8 = (bf16[4,4,16,128]{3,2,1,0:T(8,128)(2,1)S(1)}, bf16[4,4,16,128]{3,2,1,0:T(8,128)(2,1)}, u32[]{:S(2)}) copy-start(bf16[4,4,16,128]{3,2,1,0:T(8,128)(2,1)} %copy-done.7) | copy-start | bytes 196612
  97.9 7.9 %all-to-all-start.5 = ((f32[4,4,16,128]{3,2,0,1:T(8,128)}), f32[4,4,16,128]{3,2,0,1:T(8,128)S(1)}, u32[]{:S(2)}, u32[]{:S(2)}) async-start(f32[4,4,16,128]{3,2,0,1:T(8,128)} %copy.37), calls=%async_computation.5 | async-start | bytes 262144 | tf_op jit(solution)/shard_map/all_to_all | solution.py:122
  105.8 10.8 %all-to-all-start.8 = ((bf16[4,128,128]{2,0,1:T(4,128)(2,1)}), bf16[4,128,128]{2,0,1:T(4,128)(2,1)S(1)}, u32[]{:S(2)}, u32[]{:S(2)}) async-start(bf16[4,128,128]{2,0,1:T(4,128)(2,1)} %copy.45), calls=%async_computation.8 | async-start | bytes 262144 | tf_op jit(solution)/shard_map/all_to_all | solution.py:137
  116.6 10.7 %all-to-all-start.6 = ((bf16[4,128,128]{2,0,1:T(4,128)(2,1)}), bf16[4,128,128]{2,0,1:T(4,128)(2,1)S(1)}, u32[]{:S(2)}, u32[]{:S(2)}) async-start(bf16[4,128,128]{2,0,1:T(4,128)(2,1)} %copy.40), calls=%async_computation.6 | async-start | bytes 262144 | tf_op jit(solution)/shard_map/all_to_all | solution.py:136
  127.2 26.9 %all-to-all-start.4 = ((bf16[4,1024,128]{2,0,1:T(4,128)(2,1)}), bf16[4,1024,128]{2,0,1:T(4,128)(2,1)S(1)}, u32[]{:S(2)}, u32[]{:S(2)}) async-start(bf16[4,1024,128]{2,0,1:T(4,128)(2,1)} %copy.35), calls=%async_computation.4 | async-start | bytes 2097152 | tf_op jit(solution)/shard_map/all_to_all | solution.py:135
where the time goes:
time: 156 us; the launch traced here: 155 us
  waiting for transfers between devices  59.4 us (38%)
  blocking collectives  46 us (29%)
  starting transfers between devices  20.6 us (13%)
  local copies, waits for them, and re-layouts  12.4 us (8%)
  matrix products  12.4 us (8%)
  other arithmetic  3.66 us (2%)
    all_to_all x1, blocking collectives, body(): lax.all_to_all(packed_query, 'ulysses', split_axis=0, concat_axis=1, tile...  31.4 us
    all_to_all x1, waiting for transfers between devices, body(): lax.all_to_all(packed_grad, 'ulysses', split_axis=0, concat_axis=1, tiled...  23.6 us
    all_to_all x1, waiting for transfers between devices, body(): lax.all_to_all(query_out, 'ulysses', split_axis=1, concat_axis=0, tiled=T...  21.9 us
    all_to_all x1, blocking collectives, body(): lax.all_to_all(jnp.take(block_keys, requested, axis=1), 'blk', split_axis...  8.16 us
    all_to_all x1, blocking collectives, body(): lax.all_to_all(jnp.take(block_values, requested, axis=1), 'blk', split_ax...  6.47 us
    all_to_all x1, waiting for transfers between devices, body(): lax.all_to_all(value_share, 'ulysses', split_axis=1, concat_axis=0, tiled...  6.08 us
    all_to_all x1, waiting for transfers between devices, body(): lax.all_to_all(key_share, 'ulysses', split_axis=1, concat_axis=0, tiled=T...  4.52 us
    sub x1, matrix products, attend(): expsum = jnp.where(visible, jnp.exp(scores - row_max), 0.0)  4.49 us
  transfers between devices with their start and end apart: 6, of which 5 were waited for; matrix products, arithmetic and copies ran while one was open for 10% of the time, Pallas kernels for 0%

commit v1 on v0

--- a/solution.py
+++ b/solution.py
@@ -5,6 +5,28 @@
 from jax.sharding import PartitionSpec as P
 
 KB = 16
+
+
+def split_up(shard, dim, peers):
+    before, after = (shard.shape[:dim], shard.shape[dim + 1 :])
+    return jnp.moveaxis(shard.reshape(*before, peers, -1, *after), dim, 0)
+
+
+def joined_along(tiles, dim):
+    shape = list(tiles.shape[1:])
+    shape[dim] *= tiles.shape[0]
+    return jnp.moveaxis(tiles, 0, dim).reshape(shape)
+
+
+def pairwise_exchange(x, axis, split_dim, concat_dim):
+    peers, position = (lax.axis_size(axis), lax.axis_index(axis))
+    tiles = split_up(x, split_dim, peers)
+    outs = [tiles[position]]
+    for step in range(1, peers):
+        sent = tiles[position ^ step]
+        outs.append(lax.ppermute(sent, axis, [(i, i ^ step) for i in range(peers)]))
+    tiles = jnp.stack(outs)[position ^ jnp.arange(peers)]
+    return joined_along(tiles, concat_dim)
 
 
 def body(query_rows, out_grad, key_rows, value_rows, routes):
@@ -24,7 +46,7 @@
     packed_query = query_rows.reshape(head_count * sub_count, sub_length, head_dim)
     packed_grad = out_grad.reshape(head_count * sub_count, sub_length, head_dim)
     local_query, local_grad = (
-        lax.all_to_all(packed_query, "ulysses", split_axis=0, concat_axis=1, tiled=True),
+        pairwise_exchange(packed_query, "ulysses", 0, 1),
         lax.all_to_all(packed_grad, "ulysses", split_axis=0, concat_axis=1, tiled=True),
     )
     first_head = my_rank * item_count // sub_count

time: 156 us -> 149 us (0.955)
  blocking collectives: 46 us -> 0 us
  starting transfers between devices: 20.6 us -> 51.5 us
  local copies, waits for them, and re-layouts: 12.4 us -> 17 us
  waiting for transfers between devices: 59.4 us -> 62.8 us
    all_to_all x3 -> x0, blocking collectives: 46 us -> none  [the longest x1 31.4 us: body(): lax.all_to_all(packed_query, 'ulysses', split_axis=0, concat_axis=1, tile...]
    all_to_all x1, waiting for transfers between devices: 23.6 us -> 0.01 us  [body(): lax.all_to_all(packed_grad, 'ulysses', split_axis=0, concat_axis=1, tiled...]
    ppermute x0 -> x7, waiting for transfers between devices: none -> 21.2 us  [pairwise_exchange(): outs.append(lax.ppermute(sent, axis, [(i, i ^ step) for i in range(peers)]))]
    ppermute x0 -> x7, starting transfers between devices: none -> 14.3 us  [pairwise_exchange(): outs.append(lax.ppermute(sent, axis, [(i, i ^ step) for i in range(peers)]))]
    all_to_all x1, starting transfers between devices: 3.44 us -> 12.2 us  [body(): lax.all_to_all(value_share, 'ulysses', split_axis=1, concat_axis=0, tiled...]
    all_to_all x0 -> x2, starting transfers between devices: none -> 6.57 us  [the longest x1 3.29 us: body(): lax.all_to_all(jnp.take(block_values, requested, axis=1), 'blk', split_ax...]
    all_to_all x0 -> x2, waiting for transfers between devices: none -> 5.93 us  [the longest x1 3.83 us: body(): lax.all_to_all(jnp.take(block_keys, requested, axis=1), 'blk', split_axis...]
  transfers between devices with their start and end apart: 6 -> 15, of which waited for: 5 -> 8; matrix products, arithmetic and copies ran while one was open for 10% -> 18% of each run, Pallas kernels for 0% -> 0%
where the time goes in v1:
time: 149 us; the launch traced here: 148 us
  waiting for transfers between devices  62.8 us (42%)
  starting transfers between devices  51.5 us (35%)
  local copies, waits for them, and re-layouts  17 us (11%)
  matrix products  12.1 us (8%)
  other arithmetic  3.41 us (2%)
    all_to_all x1, waiting for transfers between devices, body(): lax.all_to_all(query_out, 'ulysses', split_axis=1, concat_axis=0, tiled=T...  21.7 us
    ppermute x7, waiting for transfers between devices, pairwise_exchange(): outs.append(lax.ppermute(sent, axis, [(i, i ^ step) for i in range(peers)]))  21.2 us
    ppermute x7, starting transfers between devices, pairwise_exchange(): outs.append(lax.ppermute(sent, axis, [(i, i ^ step) for i in range(peers)]))  14.3 us
    all_to_all x1, starting transfers between devices, body(): lax.all_to_all(value_share, 'ulysses', split_axis=1, concat_axis=0, tiled...  12.2 us
    all_to_all x1, waiting for transfers between devices, body(): lax.all_to_all(value_share, 'ulysses', split_axis=1, concat_axis=0, tiled...  6.08 us
    all_to_all x1, starting transfers between devices, body(): lax.all_to_all(packed_grad, 'ulysses', split_axis=0, concat_axis=1, tiled...  4.88 us
    all_to_all x1, waiting for transfers between devices, body(): lax.all_to_all(key_share, 'ulysses', split_axis=1, concat_axis=0, tiled=T...  4.52 us
    sub x1, matrix products, attend(): expsum = jnp.where(visible, jnp.exp(scores - row_max), 0.0)  4.22 us
  transfers between devices with their start and end apart: 15, of which 8 were waited for; matrix products, arithmetic and copies ran while one was open for 18% of the time, Pallas kernels for 0%

profile of v1, /device:TPU:0, one launch (start us, length us, event | category | flops | bytes accessed | tf_op | source)
XLA Modules:
  0.0 147.9 jit_solution(3814734142644426341)
XLA Ops:
  2.1 3.1 %collective-permute-start = (bf16[4,128,128]{2,1,0:T(8,128)(2,1)S(1)}, bf16[4,128,128]{2,1,0:T(8,128)(2,1)S(1)}, u32[]{:S(2)}, u32[]{:S(2)}) collective-permute-start(bf16[4,128,128]{2,1,0:T(8,128)(2,1)S(1)} %get-tuple-element.34), channel_id=1, source_target_pairs={{0,1},{1,0},{2,3},{3,2},{4,5},{5,4},{6,7},{7,6},{8,9},{9,8},{10,11... | collective-permute-start | bytes 393224 | tf_op jit(solution)/shard_map/ppermute | solution.py:27
  6.7 3.0 %collective-permute-start.3 = (bf16[4,128,128]{2,1,0:T(8,128)(2,1)S(1)}, bf16[4,128,128]{2,1,0:T(8,128)(2,1)S(1)}, u32[]{:S(2)}, u32[]{:S(2)}) collective-permute-start(bf16[4,128,128]{2,1,0:T(8,128)(2,1)S(1)} %get-tuple-element.31), channel_id=1, source_target_pairs={{0,4},{1,5},{2,6},{3,7},{4,0},{5,1},{6,2},{7,3},{8,12},{9,13},{10,... | collective-permute-start | bytes 393224 | tf_op jit(solution)/shard_map/ppermute | solution.py:27
  14.1 3.3 %all-to-all-start = ((bf16[4,4,16,128]{3,2,0,1:T(8,128)(2,1)}), bf16[4,4,16,128]{3,2,0,1:T(8,128)(2,1)S(1)}, u32[]{:S(2)}, u32[]{:S(2)}) async-start(bf16[4,4,16,128]{3,2,0,1:T(8,128)(2,1)} %get-tuple-element.49), calls=%async_computation | async-start | bytes 131072 | tf_op jit(solution)/shard_map/all_to_all | solution.py:60
  17.6 3.8 %all-to-all-done = bf16[4,4,16,128]{3,2,0,1:T(8,128)(2,1)S(1)} async-done(((bf16[4,4,16,128]{3,2,0,1:T(8,128)(2,1)}), bf16[4,4,16,128]{3,2,0,1:T(8,128)(2,1)S(1)}, u32[]{:S(2)}, u32[]{:S(2)}) %all-to-all-start) | async-done | bytes 65568 | tf_op jit(solution)/shard_map/all_to_all | solution.py:60
  21.5 3.3 %all-to-all-start.1 = ((bf16[4,4,16,128]{3,2,0,1:T(8,128)(2,1)}), bf16[4,4,16,128]{3,2,0,1:T(8,128)(2,1)S(1)}, u32[]{:S(2)}, u32[]{:S(2)}) async-start(bf16[4,4,16,128]{3,2,0,1:T(8,128)(2,1)} %get-tuple-element.48), calls=%async_computation.1 | async-start | bytes 131072 | tf_op jit(solution)/shard_map/all_to_all | solution.py:63
  26.7 2.1 %all-to-all-done.1 = bf16[4,4,16,128]{3,2,0,1:T(8,128)(2,1)S(1)} async-done(((bf16[4,4,16,128]{3,2,0,1:T(8,128)(2,1)}), bf16[4,4,16,128]{3,2,0,1:T(8,128)(2,1)S(1)}, u32[]{:S(2)}, u32[]{:S(2)}) %all-to-all-start.1) | async-done | bytes 65568 | tf_op jit(solution)/shard_map/all_to_all | solution.py:63
  28.8 4.9 %all-to-all-start.2 = ((bf16[32,128,128]{2,1,0:T(8,128)(2,1)}), bf16[32,128,128]{2,1,0:T(8,128)(2,1)}, u32[]{:S(2)}, u32[]{:S(2)}) async-start(bf16[32,128,128]{2,1,0:T(8,128)(2,1)} %param.8), calls=%async_computation.2 | async-start | bytes 2097152 | tf_op jit(solution)/shard_map/all_to_all | solution.py:50
  34.4 3.8 %collective-permute-start.5 = (bf16[4,128,128]{2,1,0:T(8,128)(2,1)S(1)}, bf16[4,128,128]{2,1,0:T(8,128)(2,1)S(1)}, u32[]{:S(2)}, u32[]{:S(2)}) collective-permute-start(bf16[4,128,128]{2,1,0:T(8,128)(2,1)S(1)} %get-tuple-element.29), channel_id=1, source_target_pairs={{0,6},{1,7},{2,4},{3,5},{4,2},{5,3},{6,0},{7,1},{8,14},{9,15},{10,... | collective-permute-start | bytes 393224 | tf_op jit(solution)/shard_map/ppermute | solution.py:27
  39.9 18.9 %collective-permute-done.5 = bf16[4,128,128]{2,1,0:T(8,128)(2,1)S(1)} collective-permute-done((bf16[4,128,128]{2,1,0:T(8,128)(2,1)S(1)}, bf16[4,128,128]{2,1,0:T(8,128)(2,1)S(1)}, u32[]{:S(2)}, u32[]{:S(2)}) %collective-permute-start.5) | collective-permute-done | bytes 131104 | tf_op jit(solution)/shard_map/ppermute | solution.py:27
  58.8 2.3 %collective-permute-done.6 = bf16[4,128,128]{2,1,0:T(8,128)(2,1)S(1)} collective-permute-done((bf16[4,128,128]{2,1,0:T(8,128)(2,1)S(1)}, bf16[4,128,128]{2,1,0:T(8,128)(2,1)S(1)}, u32[]{:S(2)}, u32[]{:S(2)}) %collective-permute-start.6) | collective-permute-done | bytes 131104 | tf_op jit(solution)/shard_map/ppermute | solution.py:27
  62.0 4.2 %fusion.43 = (f32[4,1024]{1,0:T(4,128)S(1)}, f32[4,1024,192]{1,2,0:T(8,128)}) fusion(pred[4,1024,128]{1,2,0:T(32,128)(4,1)S(1)} %broadcast_compare_fusion, pred[192]{0:T(512)(128)(4,1)S(1)} %pad.5.clone, bf16[4,1024,128]{2,1,0:T(8,128)(2,1)S(1)} %bitcast.88, bf16[4,64,128]{2,1,0:T(8,128)(2,1)} %bitcast.105, bf16[4,128,128]{2,1,0:T(8,128)(2,1)S(1)} %get-tuple-element.53), kind=kOutput, calls=%fused_computation.88 | convolution fusion | flops 409731264 | bytes 4931776 | tf_op jit(solution)/shard_map/while/body/eval_jaxpr/sub | solution.py:107
  66.2 2.3 %fusion.9 = bf16[4,1024,192]{1,2,0:T(8,128)(2,1)S(1)} fusion(f32[4,1024,192]{1,2,0:T(8,128)} %get-tuple-element.51, f32[4,1024]{1,0:T(4,128)S(1)} %get-tuple-element.50), kind=kLoop, calls=%fused_computation.17 | loop fusion | flops 1572864 | bytes 4734976 | tf_op jit(solution)/shard_map/while/body/eval_jaxpr/convert_element_type | solution.py:109
  72.1 3.3 %all-to-all-start.6 = ((f32[4,4,16,128]{3,2,0,1:T(8,128)}), f32[4,4,16,128]{3,2,0,1:T(8,128)S(1)}, u32[]{:S(2)}, u32[]{:S(2)}) async-start(f32[4,4,16,128]{3,2,0,1:T(8,128)} %copy.42), calls=%async_computation.6 | async-start | bytes 262144 | tf_op jit(solution)/shard_map/all_to_all | solution.py:145
  75.5 2.5 %multiply_reduce_fusion = f32[4,1024]{1,0:T(4,128)S(1)} fusion(bf16[4,1024,128]{2,1,0:T(8,128)(2,1)} %bitcast.91, bf16[4,1024,192]{1,2,0:T(8,128)(2,1)S(1)} %fusion.9, bf16[4,64,128]{2,1,0:T(8,128)(2,1)S(1)} %bitcast.107, bf16[4,128,128]{2,1,0:T(8,128)(2,1)S(1)} %get-tuple-element.52), kind=kOutput, calls=%fused_computation.12 | convolution fusion | flops 203288576 | bytes 2834432 | tf_op jit(solution)/shard_map/while/body/eval_jaxpr/irk,ikd->ird/dot_general | solution.py:110
  78.0 2.5 %fusion.1 = bf16[4,1024,192]{1,2,0:T(8,128)(2,1)S(1)} fusion(bf16[4,1024,128]{2,1,0:T(8,128)(2,1)S(1)} %bitcast.92, f32[4,1024]{1,0:T(4,128)S(1)} %multiply_reduce_fusion, f32[4,1024,192]{1,2,0:T(8,128)} %get-tuple-element.51, f32[4,1024]{1,0:T(4,128)S(1)} %get-tuple-element.50, bf16[4,64,128]{2,1,0:T(8,128)(2,1)S(1)} %bitcast.108, ...), kind=kOutput, calls=%fused_computation.5 | convolution fusion | flops 204865536 | bytes 5996544 | tf_op jit(solution)/shard_map/while/body/eval_jaxpr/ird,ikd->irk/dot_general | solution.py:114
  81.7 3.3 %all-to-all-start.4 = ((f32[4,4,16,128]{3,2,0,1:T(8,128)}), f32[4,4,16,128]{3,2,0,1:T(8,128)S(1)}, u32[]{:S(2)}, u32[]{:S(2)}) async-start(f32[4,4,16,128]{3,2,0,1:T(8,128)} %copy.37), calls=%async_computation.4 | async-start | bytes 262144 | tf_op jit(solution)/shard_map/all_to_all | solution.py:144
  86.3 3.3 %all-to-all-done.4 = f32[4,4,16,128]{3,2,0,1:T(8,128)S(1)} async-done(((f32[4,4,16,128]{3,2,0,1:T(8,128)}), f32[4,4,16,128]{3,2,0,1:T(8,128)S(1)}, u32[]{:S(2)}, u32[]{:S(2)}) %all-to-all-start.4) | async-done | bytes 131104 | tf_op jit(solution)/shard_map/all_to_all | solution.py:144
  89.6 12.2 %all-to-all-start.7 = ((bf16[4,128,128]{2,0,1:T(4,128)(2,1)}), bf16[4,128,128]{2,0,1:T(4,128)(2,1)S(1)}, u32[]{:S(2)}, u32[]{:S(2)}) async-start(bf16[4,128,128]{2,0,1:T(4,128)(2,1)} %copy.45), calls=%async_computation.7 | async-start | bytes 262144 | tf_op jit(solution)/shard_map/all_to_all | solution.py:159
  103.2 6.1 %all-to-all-done.7 = bf16[4,128,128]{2,0,1:T(4,128)(2,1)S(1)} async-done(((bf16[4,128,128]{2,0,1:T(4,128)(2,1)}), bf16[4,128,128]{2,0,1:T(4,128)(2,1)S(1)}, u32[]{:S(2)}, u32[]{:S(2)}) %all-to-all-start.7) | async-done | bytes 131104 | tf_op jit(solution)/shard_map/all_to_all | solution.py:159
  109.2 3.4 %all-to-all-start.5 = ((bf16[4,128,128]{2,0,1:T(4,128)(2,1)}), bf16[4,128,128]{2,0,1:T(4,128)(2,1)S(1)}, u32[]{:S(2)}, u32[]{:S(2)}) async-start(bf16[4,128,128]{2,0,1:T(4,128)(2,1)} %copy.40), calls=%async_computation.5 | async-start | bytes 262144 | tf_op jit(solution)/shard_map/all_to_all | solution.py:158
  113.6 1.8 %copy.35 = bf16[4,1024,128]{2,0,1:T(4,128)(2,1)} copy(bf16[4,1024,128]{2,1,0:T(8,128)(2,1)S(1)} %multiply_convert_fusion) | data formatting | bytes 2097152 | tf_op jit(solution)/shard_map/while/body/eval_jaxpr/convert_element_type | solution.py:121
  115.4 4.5 %all-to-all-done.5 = bf16[4,128,128]{2,0,1:T(4,128)(2,1)S(1)} async-done(((bf16[4,128,128]{2,0,1:T(4,128)(2,1)}), bf16[4,128,128]{2,0,1:T(4,128)(2,1)S(1)}, u32[]{:S(2)}, u32[]{:S(2)}) %all-to-all-start.5) | async-done | bytes 131104 | tf_op jit(solution)/shard_map/all_to_all | solution.py:158
  119.9 3.6 %all-to-all-start.3 = ((bf16[4,1024,128]{2,0,1:T(4,128)(2,1)}), bf16[4,1024,128]{2,0,1:T(4,128)(2,1)S(1)}, u32[]{:S(2)}, u32[]{:S(2)}) async-start(bf16[4,1024,128]{2,0,1:T(4,128)(2,1)} %copy.35), calls=%async_computation.3 | async-start | bytes 2097152 | tf_op jit(solution)/shard_map/all_to_all | solution.py:157
  125.0 21.7 %all-to-all-done.3 = bf16[4,1024,128]{2,0,1:T(4,128)(2,1)S(1)} async-done(((bf16[4,1024,128]{2,0,1:T(4,128)(2,1)}), bf16[4,1024,128]{2,0,1:T(4,128)(2,1)S(1)}, u32[]{:S(2)}, u32[]{:S(2)}) %all-to-all-start.3) | async-done | bytes 1048608 | tf_op jit(solution)/shard_map/all_to_all | solution.py:157
  (75 shorter events, 23.6 us)
Async XLA Ops:
  0.6 10.3 %copy-start = (s32[4,4]{1,0:T(4,128)S(1)}, s32[4,4]{1,0:T(4,128)}, u32[]{:S(2)}) copy-start(s32[4,4]{1,0:T(4,128)} %param.11) | copy-start | bytes 196
  2.1 32.3 %collective-permute-start = (bf16[4,128,128]{2,1,0:T(8,128)(2,1)S(1)}, bf16[4,128,128]{2,1,0:T(8,128)(2,1)S(1)}, u32[]{:S(2)}, u32[]{:S(2)}) collective-permute-start(bf16[4,128,128]{2,1,0:T(8,128)(2,1)S(1)} %get-tuple-element.34), channel_id=1, source_target_pairs={{0,1},{1,0},{2,3},{3,2},{4,5},{5,4},{6,7},{7,6},{8,9},{9,8},{10,11... | collective-permute-start | bytes 393224 | tf_op jit(solution)/shard_map/ppermute | solution.py:27
  5.1 33.1 %collective-permute-start.1 = (bf16[4,128,128]{2,1,0:T(8,128)(2,1)S(1)}, bf16[4,128,128]{2,1,0:T(8,128)(2,1)S(1)}, u32[]{:S(2)}, u32[]{:S(2)}) collective-permute-start(bf16[4,128,128]{2,1,0:T(8,128)(2,1)S(1)} %get-tuple-element.33), channel_id=1, source_target_pairs={{0,2},{1,3},{2,0},{3,1},{4,6},{5,7},{6,4},{7,5},{8,10},{9,11},{10,... | collective-permute-start | bytes 393224 | tf_op jit(solution)/shard_map/ppermute | solution.py:27
  6.7 33.1 %collective-permute-start.2 = (bf16[4,128,128]{2,1,0:T(8,128)(2,1)S(1)}, bf16[4,128,128]{2,1,0:T(8,128)(2,1)S(1)}, u32[]{:S(2)}, u32[]{:S(2)}) collective-permute-start(bf16[4,128,128]{2,1,0:T(8,128)(2,1)S(1)} %get-tuple-element.32), channel_id=1, source_target_pairs={{0,3},{1,2},{2,1},{3,0},{4,7},{5,6},{6,5},{7,4},{8,11},{9,10},{10,... | collective-permute-start | bytes 393224 | tf_op jit(solution)/shard_map/ppermute | solution.py:27
  6.7 33.1 %collective-permute-start.3 = (bf16[4,128,128]{2,1,0:T(8,128)(2,1)S(1)}, bf16[4,128,128]{2,1,0:T(8,128)(2,1)S(1)}, u32[]{:S(2)}, u32[]{:S(2)}) collective-permute-start(bf16[4,128,128]{2,1,0:T(8,128)(2,1)S(1)} %get-tuple-element.31), channel_id=1, source_target_pairs={{0,4},{1,5},{2,6},{3,7},{4,0},{5,1},{6,2},{7,3},{8,12},{9,13},{10,... | collective-permute-start | bytes 393224 | tf_op jit(solution)/shard_map/ppermute | solution.py:27
  9.7 30.2 %collective-permute-start.4 = (bf16[4,128,128]{2,1,0:T(8,128)(2,1)S(1)}, bf16[4,128,128]{2,1,0:T(8,128)(2,1)S(1)}, u32[]{:S(2)}, u32[]{:S(2)}) collective-permute-start(bf16[4,128,128]{2,1,0:T(8,128)(2,1)S(1)} %get-tuple-element.30), channel_id=1, source_target_pairs={{0,5},{1,4},{2,7},{3,6},{4,1},{5,0},{6,3},{7,2},{8,13},{9,12},{10,... | collective-permute-start | bytes 393224 | tf_op jit(solution)/shard_map/ppermute | solution.py:27
  12.2 49.8 %copy-start.3 = (bf16[4,128,128]{2,1,0:T(8,128)(2,1)}, bf16[4,128,128]{2,1,0:T(8,128)(2,1)S(1)}, u32[]{:S(2)}) copy-start(bf16[4,128,128]{2,1,0:T(8,128)(2,1)S(1)} %get-tuple-element.53) | copy-start | bytes 393220
  14.1 7.4 %all-to-all-start = ((bf16[4,4,16,128]{3,2,0,1:T(8,128)(2,1)}), bf16[4,4,16,128]{3,2,0,1:T(8,128)(2,1)S(1)}, u32[]{:S(2)}, u32[]{:S(2)}) async-start(bf16[4,4,16,128]{3,2,0,1:T(8,128)(2,1)} %get-tuple-element.49), calls=%async_computation | async-start | bytes 131072 | tf_op jit(solution)/shard_map/all_to_all | solution.py:60
  21.5 7.4 %all-to-all-start.1 = ((bf16[4,4,16,128]{3,2,0,1:T(8,128)(2,1)}), bf16[4,4,16,128]{3,2,0,1:T(8,128)(2,1)S(1)}, u32[]{:S(2)}, u32[]{:S(2)}) async-start(bf16[4,4,16,128]{3,2,0,1:T(8,128)(2,1)} %get-tuple-element.48), calls=%async_computation.1 | async-start | bytes 131072 | tf_op jit(solution)/shard_map/all_to_all | solution.py:63
  28.8 39.7 %all-to-all-start.2 = ((bf16[32,128,128]{2,1,0:T(8,128)(2,1)}), bf16[32,128,128]{2,1,0:T(8,128)(2,1)}, u32[]{:S(2)}, u32[]{:S(2)}) async-start(bf16[32,128,128]{2,1,0:T(8,128)(2,1)} %param.8), calls=%async_computation.2 | async-start | bytes 2097152 | tf_op jit(solution)/shard_map/all_to_all | solution.py:50
  34.4 24.5 %collective-permute-start.5 = (bf16[4,128,128]{2,1,0:T(8,128)(2,1)S(1)}, bf16[4,128,128]{2,1,0:T(8,128)(2,1)S(1)}, u32[]{:S(2)}, u32[]{:S(2)}) collective-permute-start(bf16[4,128,128]{2,1,0:T(8,128)(2,1)S(1)} %get-tuple-element.29), channel_id=1, source_target_pairs={{0,6},{1,7},{2,4},{3,5},{4,2},{5,3},{6,0},{7,1},{8,14},{9,15},{10,... | collective-permute-start | bytes 393224 | tf_op jit(solution)/shard_map/ppermute | solution.py:27
  38.2 22.9 %collective-permute-start.6 = (bf16[4,128,128]{2,1,0:T(8,128)(2,1)S(1)}, bf16[4,128,128]{2,1,0:T(8,128)(2,1)S(1)}, u32[]{:S(2)}, u32[]{:S(2)}) collective-permute-start(bf16[4,128,128]{2,1,0:T(8,128)(2,1)S(1)} %get-tuple-element.28), channel_id=1, source_target_pairs={{0,7},{1,6},{2,5},{3,4},{4,3},{5,2},{6,1},{7,0},{8,15},{9,14},{10,... | collective-permute-start | bytes 393224 | tf_op jit(solution)/shard_map/ppermute | solution.py:27
  68.5 6.9 %copy-start.6 = (bf16[4,4,16,128]{3,2,1,0:T(8,128)(2,1)S(1)}, bf16[4,4,16,128]{3,2,1,0:T(8,128)(2,1)}, u32[]{:S(2)}) copy-start(bf16[4,4,16,128]{3,2,1,0:T(8,128)(2,1)} %copy.32) | copy-start | bytes 196612
  69.9 1.0 copy-start.1
  72.1 9.6 %all-to-all-start.6 = ((f32[4,4,16,128]{3,2,0,1:T(8,128)}), f32[4,4,16,128]{3,2,0,1:T(8,128)S(1)}, u32[]{:S(2)}, u32[]{:S(2)}) async-start(f32[4,4,16,128]{3,2,0,1:T(8,128)} %copy.42), calls=%async_computation.6 | async-start | bytes 262144 | tf_op jit(solution)/shard_map/all_to_all | solution.py:145
  75.4 2.5 %copy-start.2 = (bf16[8,4,128,128]{3,2,0,1:T(8,128)(2,1)S(1)}, bf16[8,4,128,128]{3,2,0,1:T(8,128)(2,1)}, u32[]{:S(2)}) copy-start(bf16[8,4,128,128]{3,2,0,1:T(8,128)(2,1)} %copy-done.1) | copy-start | bytes 3145732
  81.0 31.6 %copy-start.4 = (bf16[4,128,128]{2,1,0:T(8,128)(2,1)S(1)}, bf16[4,128,128]{2,1,0:T(8,128)(2,1)}, u32[]{:S(2)}) copy-start(bf16[4,128,128]{2,1,0:T(8,128)(2,1)} %copy-done.3) | copy-start | bytes 393220
  81.0 31.6 %copy-start.5 = (bf16[4,4,16,128]{3,2,1,0:T(8,128)(2,1)S(1)}, bf16[4,4,16,128]{3,2,1,0:T(8,128)(2,1)}, u32[]{:S(2)}) copy-start(bf16[4,4,16,128]{3,2,1,0:T(8,128)(2,1)} %copy.31) | copy-start | bytes 196612
  81.7 7.9 %all-to-all-start.4 = ((f32[4,4,16,128]{3,2,0,1:T(8,128)}), f32[4,4,16,128]{3,2,0,1:T(8,128)S(1)}, u32[]{:S(2)}, u32[]{:S(2)}) async-start(f32[4,4,16,128]{3,2,0,1:T(8,128)} %copy.37), calls=%async_computation.4 | async-start | bytes 262144 | tf_op jit(solution)/shard_map/all_to_all | solution.py:144
  89.6 19.6 %all-to-all-start.7 = ((bf16[4,128,128]{2,0,1:T(4,128)(2,1)}), bf16[4,128,128]{2,0,1:T(4,128)(2,1)S(1)}, u32[]{:S(2)}, u32[]{:S(2)}) async-start(bf16[4,128,128]{2,0,1:T(4,128)(2,1)} %copy.45), calls=%async_computation.7 | async-start | bytes 262144 | tf_op jit(solution)/shard_map/all_to_all | solution.py:159
  109.2 10.7 %all-to-all-start.5 = ((bf16[4,128,128]{2,0,1:T(4,128)(2,1)}), bf16[4,128,128]{2,0,1:T(4,128)(2,1)S(1)}, u32[]{:S(2)}, u32[]{:S(2)}) async-start(bf16[4,128,128]{2,0,1:T(4,128)(2,1)} %copy.40), calls=%async_computation.5 | async-start | bytes 262144 | tf_op jit(solution)/shard_map/all_to_all | solution.py:158
  119.9 26.8 %all-to-all-start.3 = ((bf16[4,1024,128]{2,0,1:T(4,128)(2,1)}), bf16[4,1024,128]{2,0,1:T(4,128)(2,1)S(1)}, u32[]{:S(2)}, u32[]{:S(2)}) async-start(bf16[4,1024,128]{2,0,1:T(4,128)(2,1)} %copy.35), calls=%async_computation.3 | async-start | bytes 2097152 | tf_op jit(solution)/shard_map/all_to_all | solution.py:157
